TPU v7x, 256 devices: a whole 4x4x8 slice. The times are simulated.
256 devices in a mesh: outer: 8 (over z_hi, y), shard: 32 (over z_lo, x, core).
Axes of the slice: x: 4, y: 4, z: 8 (z_hi: 2, z_lo: 4; z = z_hi * 4 + z_lo), core: 2. Of those that a mesh axis runs over, the one named last changes fastest.
Arguments:
- grad_values: bfloat16 [8, 32, 256, 14848], P('outer', 'shard'), may hold values from -6 to 6
- grad_scales: bfloat16 [8, 32, 256, 116], P('outer', 'shard'), may hold values from 0.029907227 to 0.29882812
- block_owner: int32 [256], replicated, may hold values from 0 to 31, as said below
- projector: bfloat16 [8192, 256], P(('outer', 'shard')), may hold values from -0.375 to 0.375
- weights: bfloat16 [8192, 14848], P(('outer', 'shard')), may hold values from -6 to 6
- first_moment: float32 [256, 14848], P('shard'), may hold values from -6 to 6
- second_moment: float32 [256, 14848], P('shard'), may hold values from 0.5 to 4
Outputs:
- new_weights: bfloat16 [8192, 14848], P(('outer', 'shard'))
- new_first: float32 [256, 14848], P('shard')
- new_second: float32 [256, 14848], P('shard')
Inputs may be any that keep to these rules, and one draw needn't show every extreme that they name: `block_owner`: every index of shard owns exactly 8 rows.
All inputs are finite; a program needn't handle non-finite values.
Results may differ from a plain program's by a relative error of at most 0.0015.
Values may be sent and summed in bfloat16 or wider, within the bound.
A program may use at most 128 MiB of HBM per device.

v0:
```python
import jax
import jax.numpy as jnp
from jax import lax
from jax.sharding import PartitionSpec as P

first_decay = 0.9
second_decay = 0.999
step_count = 100.0
update_scale = 0.25


def per_device(
    grad_values, grad_scales, block_owner, projector, weights, first_moment, second_moment
):
    shards = lax.axis_size("shard")
    rank_rows = block_owner.shape[0]
    owned_rows = rank_rows // shards
    values = grad_values[0, 0]
    scales = grad_scales[0, 0]
    col_blocks = scales.shape[1]
    block_width = values.shape[1] // col_blocks
    row_index = jnp.arange(rank_rows, dtype=jnp.int32)
    sort_keys = block_owner * rank_rows + row_index
    position = jnp.sum((sort_keys[None, :] < sort_keys[:, None]).astype(jnp.int32), axis=1)
    placing = (position[None, :] == row_index[:, None]).astype(jnp.bfloat16)
    sent_values = jnp.dot(placing, values, preferred_element_type=jnp.float32).astype(jnp.bfloat16)
    sent_scales = jnp.dot(placing, scales, preferred_element_type=jnp.float32).astype(jnp.bfloat16)
    got_values, got_scales = (
        lax.all_to_all(
            sent_values.reshape(shards, owned_rows, -1),
            "shard",
            split_axis=0,
            concat_axis=0,
            tiled=True,
        ),
        lax.all_to_all(
            sent_scales.reshape(shards, owned_rows, col_blocks),
            "shard",
            split_axis=0,
            concat_axis=0,
            tiled=True,
        ),
    )
    blocked = got_values.reshape(shards, owned_rows, col_blocks, block_width).astype(jnp.float32)
    pod_sum = jnp.sum(blocked * got_scales.astype(jnp.float32)[..., None], axis=0)
    pod_low = pod_sum.reshape(owned_rows, -1).astype(jnp.bfloat16)
    all_rows = lax.all_gather(pod_low[None], "outer", axis=0, tiled=True)
    owned = jnp.sum(all_rows.astype(jnp.float32), axis=0)
    new_first = first_decay * first_moment + (1.0 - first_decay) * owned
    new_second = second_decay * second_moment + (1.0 - second_decay) * owned * owned
    corrected = new_first / (1.0 - first_decay**step_count)
    spread = jnp.sqrt(new_second / (1.0 - second_decay**step_count)) + 1e-08
    update = (corrected / spread).astype(jnp.bfloat16)
    gathered = lax.all_gather(update, "shard", axis=0, tiled=True)
    reordered = jnp.dot(projector, placing.T, preferred_element_type=jnp.float32).astype(
        jnp.bfloat16
    )
    change = jnp.dot(reordered, gathered, preferred_element_type=jnp.float32)
    new_weights = (weights.astype(jnp.float32) - update_scale * change).astype(jnp.bfloat16)
    return (new_weights, new_first, new_second)


def solution(mesh):
    placed = (
        P("outer", "shard", None, None),
        P("outer", "shard", None, None),
        P(),
        P(("outer", "shard"), None),
        P(("outer", "shard"), None),
        P("shard", None),
        P("shard", None),
    )
    return jax.shard_map(
        per_device,
        mesh=mesh,
        in_specs=placed,
        out_specs=(P(("outer", "shard"), None), P("shard", None), P("shard", None)),
        check_vma=False,
    )
```

profile of v0, /device:TPU:1, one launch (start us, length us, event | category | flops | bytes accessed | tf_op | source)
XLA Modules:
  0.0 366.5 jit_solution(17580511060379455319)
XLA Ops:
  7.2 0.0 copy-start
  7.2 0.7 iota_add_fusion
  7.9 0.2 convert_reduce_fusion.1
  8.1 0.0 copy-done
  8.1 0.2 convolution_convert_fusion.1
  8.3 0.7 copy.13
  9.0 10.0 %all-to-all-start.1 = ((bf16[32,8,116]{2,1,0:T(8,128)(2,1)}), bf16[32,8,116]{2,1,0:T(8,128)(2,1)S(1)}, u32[]{:S(2)}, u32[]{:S(2)}) async-start(bf16[32,8,116]{2,1,0:T(8,128)(2,1)} %bitcast.3), calls=%async_computation.1 | async-start | bytes 131072 | tf_op jit(solution)/shard_map/all_to_all | solution.py:36
  19.0 8.4 %fusion = bf16[32,8,14848]{2,1,0:T(8,128)(2,1)} fusion(bf16[1,1,256,14848]{3,2,1,0:T(8,128)(2,1)} %param.7, s32[256]{0:T(256)S(1)} %convert_reduce_fusion.1), kind=kOutput, calls=%fused_computation.1 | convolution fusion | flops 1950023680 | bytes 15205376 | tf_op jit(solution)/shard_map/dot_general | solution.py:26
  27.4 0.0 all-to-all-done.1
  27.4 7.8 %all-to-all-start = ((bf16[32,8,14848]{2,1,0:T(8,128)(2,1)}), bf16[32,8,14848]{2,1,0:T(8,128)(2,1)}, u32[]{:S(2)}, u32[]{:S(2)}) async-start(bf16[32,8,14848]{2,1,0:T(8,128)(2,1)} %fusion), calls=%async_computation | async-start | bytes 15204352 | tf_op jit(solution)/shard_map/all_to_all | solution.py:29
  35.2 0.0 copy-start.2
  35.2 0.0 all-gather.6.cloned.1.call-start
  35.3 0.4 copy.14
  35.7 0.0 copy-start.1
  35.7 0.0 copy-start.3
  35.7 166.9 %all-to-all-done = bf16[32,8,14848]{2,1,0:T(8,128)(2,1)} async-done(((bf16[32,8,14848]{2,1,0:T(8,128)(2,1)}), bf16[32,8,14848]{2,1,0:T(8,128)(2,1)}, u32[]{:S(2)}, u32[]{:S(2)}) %all-to-all-start) | async-done | bytes 7602208 | tf_op jit(solution)/shard_map/all_to_all | solution.py:29
  202.7 8.6 %fusion.3 = bf16[8,14848]{1,0:T(8,128)(2,1)} fusion(bf16[32,8,14848]{2,1,0:T(8,128)(2,1)} %all-to-all-done, f32[32,8,116]{1,2,0:T(8,128)S(1)} %copy.14), kind=kLoop, calls=%fused_computation.6 | loop fusion | flops 11284480 | bytes 7958528 | tf_op jit(solution)/shard_map/reduce_sum | solution.py:45
  211.2 0.0 all-gather.6.cloned.1.call-update
  211.3 0.0 all-gather.4.cloned.1.call-start
  211.3 71.3 %all-gather.6.cloned.1.call-done = bf16[64,14848]{1,0:T(8,128)(2,1)} async-done(((bf16[8,14848]{1,0:T(8,128)(2,1)}), bf16[64,14848]{1,0:T(8,128)(2,1)}) %all-gather.6.cloned.1.call-update) | async-done | bytes 1900560 | tf_op jit(solution)/shard_map/all_gather | solution.py:47
  282.6 1.8 convert_reduce_fusion
  284.4 0.0 copy-done.2
  284.4 2.2 divide_convert_fusion
  286.6 0.0 all-gather.4.cloned.1.call-update
  286.6 67.3 %all-gather.4.cloned.1.call-done = bf16[256,14848]{1,0:T(8,128)(2,1)} async-done(((bf16[8,14848]{1,0:T(8,128)(2,1)}), bf16[256,14848]{1,0:T(8,128)(2,1)}) %all-gather.4.cloned.1.call-update) | async-done | bytes 7602192 | tf_op jit(solution)/shard_map/all_gather | solution.py:54
  353.9 0.0 copy-done.1
  353.9 0.0 copy-done.3
  353.9 5.7 %fusion.2 = bf16[32,14848]{1,0:T(8,128)(2,1)} fusion(bf16[256,14848]{1,0:T(8,128)(2,1)} %all-gather.4.cloned.1.call-done, bf16[32,14848]{1,0:T(8,128)(2,1)S(1)} %copy-done.1, bf16[32,256]{1,0:T(8,128)(2,1)S(1)} %copy-done.3, s32[256]{0:T(256)S(1)} %convert_reduce_fusion.1), kind=kOutput, calls=%fused_computation.4 | convolution fusion | flops 249438208 | bytes 9520128 | tf_op jit(solution)/shard_map/dot_general | solution.py:58
Async XLA Ops:
  7.2 0.9 copy-start
  9.0 18.4 %all-to-all-start.1 = ((bf16[32,8,116]{2,1,0:T(8,128)(2,1)}), bf16[32,8,116]{2,1,0:T(8,128)(2,1)S(1)}, u32[]{:S(2)}, u32[]{:S(2)}) async-start(bf16[32,8,116]{2,1,0:T(8,128)(2,1)} %bitcast.3), calls=%async_computation.1 | async-start | bytes 131072 | tf_op jit(solution)/shard_map/all_to_all | solution.py:36
  27.4 175.2 %all-to-all-start = ((bf16[32,8,14848]{2,1,0:T(8,128)(2,1)}), bf16[32,8,14848]{2,1,0:T(8,128)(2,1)}, u32[]{:S(2)}, u32[]{:S(2)}) async-start(bf16[32,8,14848]{2,1,0:T(8,128)(2,1)} %fusion), calls=%async_computation | async-start | bytes 15204352 | tf_op jit(solution)/shard_map/all_to_all | solution.py:29
  35.2 249.2 %copy-start.2 = (f32[8,14848]{1,0:T(8,128)S(1)}, f32[8,14848]{1,0:T(8,128)}, u32[]{:S(2)}) copy-start(f32[8,14848]{1,0:T(8,128)} %param.12) | copy-start | bytes 1425412
  35.2 247.3 %all-gather.6.cloned.1.call-start = ((), (), s32[]{:S(2)}) async-start(), calls=%async_computation.3 | async-start | bytes 2138112 | tf_op jit(solution)/shard_map/all_gather | solution.py:47
  35.7 318.2 %copy-start.1 = (bf16[32,14848]{1,0:T(8,128)(2,1)S(1)}, bf16[32,14848]{1,0:T(8,128)(2,1)}, u32[]{:S(2)}) copy-start(bf16[32,14848]{1,0:T(8,128)(2,1)} %param.11) | copy-start | bytes 2850820
  35.7 318.2 %copy-start.3 = (bf16[32,256]{1,0:T(8,128)(2,1)S(1)}, bf16[32,256]{1,0:T(8,128)(2,1)}, u32[]{:S(2)}) copy-start(bf16[32,256]{1,0:T(8,128)(2,1)} %param.10) | copy-start | bytes 49156
  211.3 142.7 %all-gather.4.cloned.1.call-start = ((), (), s32[]{:S(2)}) async-start(), calls=%async_computation.2 | async-start | bytes 7839744 | tf_op jit(solution)/shard_map/all_gather | solution.py:54
Sparse Core Ops, SparseCore 0:
  211.4 71.1 all-gather.5
  286.8 67.1 all-gather.3
where the time goes:
time: 367 us
  waiting for transfers between devices  306 us (83%)
  starting transfers between devices  17.9 us (5%)
  matrix products  14.3 us (4%)
  between operations  14.1 us (4%)
  other arithmetic  13.5 us (4%)
    all_to_all x1, waiting for transfers between devices, per_device(): lax.all_to_all(sent_values.reshape(shards, owned_rows, -1), 'shard', spli...  167 us
    all_gather x1, waiting for transfers between devices, per_device(): all_rows = lax.all_gather(pod_low[None], 'outer', axis=0, tiled=True)  71.3 us
    all_gather x1, waiting for transfers between devices, per_device(): gathered = lax.all_gather(update, 'shard', axis=0, tiled=True)  67.3 us
    all_to_all x1, starting transfers between devices, per_device(): lax.all_to_all(sent_scales.reshape(shards, owned_rows, col_blocks), 'shar...  10 us
    reduce_sum x1, other arithmetic, per_device(): jnp.sum(blocked * got_scales.astype(jnp.float32)[..., None], axis=0)  8.58 us
    dot_general x1, matrix products, per_device(): jnp.dot(placing, values, preferred_element_type=jnp.float32)  8.39 us
    all_to_all x1, starting transfers between devices, per_device(): lax.all_to_all(sent_values.reshape(shards, owned_rows, -1), 'shard', spli...  7.78 us
  transfers between devices with their start and end apart: 4, of which 3 were waited for; matrix products, arithmetic and copies ran while one was open for 2% of the time, Pallas kernels for 0%

commit v1 on v0

--- a/solution.py
+++ b/solution.py
@@ -44,7 +44,9 @@
     blocked = got_values.reshape(shards, owned_rows, col_blocks, block_width).astype(jnp.float32)
     pod_sum = jnp.sum(blocked * got_scales.astype(jnp.float32)[..., None], axis=0)
     pod_low = pod_sum.reshape(owned_rows, -1).astype(jnp.bfloat16)
-    all_rows = lax.all_gather(pod_low[None], "outer", axis=0, tiled=True)
+    block = pod_low[None]
+    repeated = jnp.stack([block] * lax.axis_size("outer"))
+    all_rows = jnp.concatenate(lax.all_to_all(repeated, "outer", 0, 0), axis=0)
     owned = jnp.sum(all_rows.astype(jnp.float32), axis=0)
     new_first = first_decay * first_moment + (1.0 - first_decay) * owned
     new_second = second_decay * second_moment + (1.0 - second_decay) * owned * owned

time: 367 us -> 346 us (0.943)
  waiting for transfers between devices: 306 us -> 234 us
  blocking collectives: 0 us -> 54.3 us
    all_gather x1 -> x0, waiting for transfers between devices: 71.3 us -> none  [per_device(): all_rows = lax.all_gather(pod_low[None], 'outer', axis=0, tiled=True)]
    all_to_all x0 -> x1, blocking collectives: none -> 54.3 us  [per_device(): all_rows = jnp.concatenate(lax.all_to_all(repeated, 'outer', 0, 0), axis=0)]
  transfers between devices with their start and end apart: 4 -> 3, of which waited for: 3 -> 2; matrix products, arithmetic and copies ran while one was open for 2% -> 3% of each run, Pallas kernels for 0% -> 0%
where the time goes in v1:
time: 346 us
  waiting for transfers between devices  234 us (68%)
  blocking collectives  54.3 us (16%)
  starting transfers between devices  17.8 us (5%)
  matrix products  14.3 us (4%)
  between operations  14.1 us (4%)
  other arithmetic  10.2 us (3%)
    all_to_all x1, waiting for transfers between devices, per_device(): lax.all_to_all(sent_values.reshape(shards, owned_rows, -1), 'shard', spli...  167 us
    all_gather x1, waiting for transfers between devices, per_device(): gathered = lax.all_gather(update, 'shard', axis=0, tiled=True)  66.6 us
    all_to_all x1, blocking collectives, per_device(): all_rows = jnp.concatenate(lax.all_to_all(repeated, 'outer', 0, 0), axis=0)  54.3 us
    all_to_all x1, starting transfers between devices, per_device(): lax.all_to_all(sent_scales.reshape(shards, owned_rows, col_blocks), 'shar...  10 us
    dot_general x1, matrix products, per_device(): jnp.dot(placing, values, preferred_element_type=jnp.float32)  8.37 us
    reduce_sum x1, other arithmetic, per_device(): jnp.sum(blocked * got_scales.astype(jnp.float32)[..., None], axis=0)  7.89 us
    all_to_all x1, starting transfers between devices, per_device(): lax.all_to_all(sent_values.reshape(shards, owned_rows, -1), 'shard', spli...  7.78 us
  transfers between devices with their start and end apart: 3, of which 2 were waited for; matrix products, arithmetic and copies ran while one was open for 3% of the time, Pallas kernels for 0%

profile of v1, /device:TPU:1, one launch (start us, length us, event | category | flops | bytes accessed | tf_op | source)
XLA Modules:
  0.0 345.7 jit_solution(13415896121396260854)
XLA Ops:
  7.2 0.0 copy-start
  7.2 0.7 iota_add_fusion
  7.9 0.2 convert_reduce_fusion.1
  8.1 0.0 copy-done
  8.1 0.2 convolution_convert_fusion.1
  8.3 0.7 copy.13
  9.0 10.0 %all-to-all-start.1 = ((bf16[32,8,116]{2,1,0:T(8,128)(2,1)}), bf16[32,8,116]{2,1,0:T(8,128)(2,1)S(1)}, u32[]{:S(2)}, u32[]{:S(2)}) async-start(bf16[32,8,116]{2,1,0:T(8,128)(2,1)} %bitcast.3), calls=%async_computation.1 | async-start | bytes 131072 | tf_op jit(solution)/shard_map/all_to_all | solution.py:36
  19.0 8.4 %fusion = bf16[32,8,14848]{2,1,0:T(8,128)(2,1)} fusion(bf16[1,1,256,14848]{3,2,1,0:T(8,128)(2,1)} %param.7, s32[256]{0:T(256)S(1)} %convert_reduce_fusion.1), kind=kOutput, calls=%fused_computation.1 | convolution fusion | flops 1950023680 | bytes 15205376 | tf_op jit(solution)/shard_map/dot_general | solution.py:26
  27.4 0.0 all-to-all-done.1
  27.4 7.8 %all-to-all-start = ((bf16[32,8,14848]{2,1,0:T(8,128)(2,1)}), bf16[32,8,14848]{2,1,0:T(8,128)(2,1)}, u32[]{:S(2)}, u32[]{:S(2)}) async-start(bf16[32,8,14848]{2,1,0:T(8,128)(2,1)} %fusion), calls=%async_computation | async-start | bytes 15204352 | tf_op jit(solution)/shard_map/all_to_all | solution.py:29
  35.2 0.0 all-gather.2.cloned.1.call-start
  35.2 0.4 copy.14
  35.7 0.0 copy-start.2
  35.7 0.0 copy-start.3
  35.7 167.0 %all-to-all-done = bf16[32,8,14848]{2,1,0:T(8,128)(2,1)} async-done(((bf16[32,8,14848]{2,1,0:T(8,128)(2,1)}), bf16[32,8,14848]{2,1,0:T(8,128)(2,1)}, u32[]{:S(2)}, u32[]{:S(2)}) %all-to-all-start) | async-done | bytes 7602208 | tf_op jit(solution)/shard_map/all_to_all | solution.py:29
  202.6 7.9 %fusion.3 = bf16[8,14848]{1,0:T(8,128)(2,1)S(1)} fusion(bf16[32,8,14848]{2,1,0:T(8,128)(2,1)} %all-to-all-done, f32[32,8,116]{1,2,0:T(8,128)S(1)} %copy.14), kind=kLoop, calls=%fused_computation.6 | loop fusion | flops 11284480 | bytes 7958528 | tf_op jit(solution)/shard_map/reduce_sum | solution.py:45
  210.5 0.0 copy-start.1
  210.5 0.0 copy-start.4
  210.5 0.1 stack.3
  210.7 54.3 %all_to_all.15 = bf16[8,1,8,14848]{3,2,1,0:T(8,128)(2,1)S(1)} all-to-all(bf16[8,1,8,14848]{3,2,1,0:T(8,128)(2,1)S(1)} %stack.3), channel_id=1, replica_groups=mesh['outer'=8,'shard'=32] {'outer'}, dimensions={0} | all-to-all | bytes 3801088 | tf_op jit(solution)/shard_map/all_to_all | solution.py:49
  265.0 0.3 convert_reduce_fusion
  265.2 0.0 copy-done.2
  265.2 0.0 copy-done.3
  265.3 1.2 divide_convert_fusion
  266.5 0.0 all-gather.2.cloned.1.call-update
  266.5 66.6 %all-gather.2.cloned.1.call-done = bf16[256,14848]{1,0:T(8,128)(2,1)} async-done(((bf16[8,14848]{1,0:T(8,128)(2,1)}), bf16[256,14848]{1,0:T(8,128)(2,1)}) %all-gather.2.cloned.1.call-update) | async-done | bytes 7602192 | tf_op jit(solution)/shard_map/all_gather | solution.py:56
  333.1 0.0 copy-done.1
  333.1 0.0 copy-done.4
  333.1 5.7 %fusion.2 = bf16[32,14848]{1,0:T(8,128)(2,1)} fusion(bf16[256,14848]{1,0:T(8,128)(2,1)} %all-gather.2.cloned.1.call-done, bf16[32,14848]{1,0:T(8,128)(2,1)S(1)} %copy-done.1, bf16[32,256]{1,0:T(8,128)(2,1)S(1)} %copy-done.4, s32[256]{0:T(256)S(1)} %convert_reduce_fusion.1), kind=kOutput, calls=%fused_computation.4 | convolution fusion | flops 249438208 | bytes 9520128 | tf_op jit(solution)/shard_map/dot_general | solution.py:60
Async XLA Ops:
  7.2 0.9 copy-start
  9.0 18.4 %all-to-all-start.1 = ((bf16[32,8,116]{2,1,0:T(8,128)(2,1)}), bf16[32,8,116]{2,1,0:T(8,128)(2,1)S(1)}, u32[]{:S(2)}, u32[]{:S(2)}) async-start(bf16[32,8,116]{2,1,0:T(8,128)(2,1)} %bitcast.3), calls=%async_computation.1 | async-start | bytes 131072 | tf_op jit(solution)/shard_map/all_to_all | solution.py:36
  27.4 175.2 %all-to-all-start = ((bf16[32,8,14848]{2,1,0:T(8,128)(2,1)}), bf16[32,8,14848]{2,1,0:T(8,128)(2,1)}, u32[]{:S(2)}, u32[]{:S(2)}) async-start(bf16[32,8,14848]{2,1,0:T(8,128)(2,1)} %fusion), calls=%async_computation | async-start | bytes 15204352 | tf_op jit(solution)/shard_map/all_to_all | solution.py:29
  35.2 297.9 %all-gather.2.cloned.1.call-start = ((), (), s32[]{:S(2)}) async-start(), calls=%async_computation.3 | async-start | bytes 7839744 | tf_op jit(solution)/shard_map/all_gather | solution.py:56
  35.7 229.6 %copy-start.2 = (f32[8,14848]{1,0:T(8,128)S(1)}, f32[8,14848]{1,0:T(8,128)}, u32[]{:S(2)}) copy-start(f32[8,14848]{1,0:T(8,128)} %param.12) | copy-start | bytes 1425412
  35.7 229.6 %copy-start.3 = (f32[8,14848]{1,0:T(8,128)S(1)}, f32[8,14848]{1,0:T(8,128)}, u32[]{:S(2)}) copy-start(f32[8,14848]{1,0:T(8,128)} %param.13) | copy-start | bytes 1425412
  210.5 122.6 %copy-start.1 = (bf16[32,14848]{1,0:T(8,128)(2,1)S(1)}, bf16[32,14848]{1,0:T(8,128)(2,1)}, u32[]{:S(2)}) copy-start(bf16[32,14848]{1,0:T(8,128)(2,1)} %param.11) | copy-start | bytes 2850820
  210.5 122.6 %copy-start.4 = (bf16[32,256]{1,0:T(8,128)(2,1)S(1)}, bf16[32,256]{1,0:T(8,128)(2,1)}, u32[]{:S(2)}) copy-start(bf16[32,256]{1,0:T(8,128)(2,1)} %param.10) | copy-start | bytes 49156
Sparse Core Ops, SparseCore 0:
  266.6 66.4 all-gather.1
